TPU v7x, 32 devices: a whole 2x2x4 slice. The times are simulated.
32 devices in a mesh: mesh: 32 (over z, y, x, core).
Axes of the slice: x: 2, y: 2, z: 4, core: 2. Of those that a mesh axis runs over, the one named last changes fastest.
Arguments:
- states: float32 [196608, 256], P('mesh'), may hold values from -30 to 30
- inv_sqrt_mass: float32 [196608], P('mesh'), may hold values from 0.25 to 1.75
- element_blocks: bfloat16 [512, 512, 512], P('mesh'), may hold values from -0.25 to 0.25
- element_nodes: int32 [512, 512], P('mesh'), may hold values from 0 to 6143, as said below
- element_counts: int32 [32], P('mesh'), may hold values from 1 to 16, as said below
- node_counts: int32 [32], replicated, may hold values from 4608 to 6144, as said below
- boundary_rows: int32 [32, 2, 384], P('mesh'), may hold values from 0 to 4607, as said below
Outputs:
- rotated: float32 [196608, 256], P('mesh')
Inputs may be any that keep to these rules, and one draw needn't show every extreme that they name: `node_counts`: live node rows of each device; some device has 6144. `element_counts`: live element slots of each device (the first slots are live); some device has 16. `element_nodes`: every entry is below its device's node count. `boundary_rows`: for each device the 768 entries are distinct rows below 4608.
All inputs are finite; a program needn't handle non-finite values.
Results may differ from a plain program's by a relative error of at most 0.0077.
Values sent between devices are 32-bit elements; how exact they have to be, the bound alone decides.
A program may use at most 128 MiB of HBM per device.

v0:
```python
import jax
import jax.numpy as jnp
from jax import lax
from jax.sharding import PartitionSpec as P


def passed_along(block, axis, distance):
    devices = range(lax.axis_size(axis))
    route = [(i - distance, i) for i in devices if i - distance in devices]
    return lax.ppermute(block, axis, route)


def body(
    states, inv_sqrt_mass, element_blocks, element_nodes, element_counts, node_counts, boundary_rows
):
    position = lax.axis_index("mesh")
    devices = lax.axis_size("mesh")
    row_total = states.shape[0]
    width = states.shape[1]
    slots = element_blocks.shape[0]
    lower_rows = boundary_rows[0, 0]
    upper_rows = boundary_rows[0, 1]
    shared = lower_rows.shape[0]
    has_below = position >= 1
    owner_vals, owner_mass = passed_along(
        (states[upper_rows], inv_sqrt_mass[upper_rows]), "mesh", 1
    )
    field = states.at[lower_rows].set(jnp.where(has_below, owner_vals, states[lower_rows]))
    mass = inv_sqrt_mass.at[lower_rows].set(
        jnp.where(has_below, owner_mass, inv_sqrt_mass[lower_rows])
    )
    live_slots = element_counts[0]
    row_index = jnp.arange(row_total)
    slot_index = jnp.arange(slots)
    slot_live = slot_index < live_slots

    def ham(values):
        scaled = (mass[:, None] * values).astype(jnp.bfloat16)
        empty = jnp.zeros((row_total, width), jnp.float32)

        def add_element(slot, total):
            rows = element_nodes[slot]

            def compute(acc):
                part = jnp.dot(
                    element_blocks[slot], scaled[rows], preferred_element_type=jnp.float32
                )
                return acc.at[rows].add(part)

            return lax.cond(slot_live[slot], compute, lambda acc: acc, total)

        local = lax.fori_loop(0, slots, add_element, empty)
        coming_up = passed_along(local[upper_rows], "mesh", 1)
        coming_down = passed_along(local[lower_rows], "mesh", -1)
        assembled = local.at[lower_rows].add(coming_up).at[upper_rows].add(coming_down)
        return mass[:, None] * assembled

    center = 0.5
    half_width = 1.5
    first = (ham(field) - center * field) / half_width
    second = 2.0 * (ham(first) - center * first) / half_width - field
    filtered = 2.0 * (ham(second) - center * second) / half_width - first
    live = row_index < node_counts[position]
    in_lower = jnp.any(row_index[:, None] == lower_rows[None, :], axis=1)
    owned = live & jnp.logical_not(in_lower & has_below)
    weighted = jnp.where(owned[:, None], filtered, 0.0)
    partial_value = lax.dot_general(
        weighted,
        weighted,
        (((0,), (0,)), ((), ())),
        precision=lax.Precision.HIGHEST,
        preferred_element_type=jnp.float32,
    )
    gram = lax.psum(partial_value, "mesh")
    total = (jnp.sum(node_counts) - shared * (devices - 1)).astype(jnp.float32)
    gram = gram / total
    factor = jnp.linalg.cholesky(gram)
    inverse = jax.scipy.linalg.solve_triangular(
        factor, jnp.eye(width, dtype=jnp.float32), lower=True
    )
    rotated = jnp.dot(
        filtered, inverse.T, precision=lax.Precision.HIGHEST, preferred_element_type=jnp.float32
    )
    return jnp.where(live[:, None], rotated, 0.0)


def solution(mesh):
    in_specs = (
        P("mesh", None),
        P("mesh"),
        P("mesh", None, None),
        P("mesh", None),
        P("mesh"),
        P(),
        P("mesh", None, None),
    )
    out_specs = P("mesh", None)
    return jax.shard_map(body, mesh=mesh, in_specs=in_specs, out_specs=out_specs, check_vma=False)
```

profile of v0, /device:TPU:0, one launch (start us, length us, event | category | flops | bytes accessed | tf_op | source)
XLA Modules:
  0.0 1117.1 jit_solution(17529059180484307456)
XLA Ops:
  49.4 75.4 %while.49 = (s32[]{:T(128)}, f32[6144,256]{1,0:T(8,128)}, pred[16]{0:T(512)(128)(4,1)S(1)}, s32[16,512]{1,0:T(8,128)}, bf16[16,512,512]{2,1,0:T(8,128)(2,1)}, /*index=5*/bf16[6144,256]{1,0:T(8,128)(2,1)S(1)}, s32[]{:T(128)}) while((s32[]{:T(128)}, f32[6144,256]{1,0:T(8,128)}, pred[16]{0:T(512)(128)(4,1)S(1)}, s32[16,512]{1,0:T(8,128)}, ...), condition=%wide.region_6.7_spmd, body=%wide.region_2.6_spmd.sunk | while | flops 134351360 | bytes 3422386 | solution.py:52
  50.7 13.8 %conditional.6 = (f32[6144,256]{1,0:T(8,128)}) conditional(s32[]{:T(128)} %bitcast.62, f32[6144,256]{1,0:T(8,128)} %get-tuple-element.664, (s32[16,512]{1,0:T(8,128)}, s32[]{:T(128)}, bf16[16,512,512]{2,1,0:T(8,128)(2,1)}, bf16[6144,256]{1,0:T(8,128)(2,1)S(1)}, f32[6144,256]{1,0:T(8,128)}) %tuple.128), branch_computations={%region_3.3_spmd, %region_4.5_spmd} | conditional | flops 134351360 | bytes 3422258 | solution.py:50
  65.7 13.8 %conditional.6 = (f32[6144,256]{1,0:T(8,128)}) conditional(s32[]{:T(128)} %bitcast.62, f32[6144,256]{1,0:T(8,128)} %get-tuple-element.664, (s32[16,512]{1,0:T(8,128)}, s32[]{:T(128)}, bf16[16,512,512]{2,1,0:T(8,128)(2,1)}, bf16[6144,256]{1,0:T(8,128)(2,1)S(1)}, f32[6144,256]{1,0:T(8,128)}) %tuple.128), branch_computations={%region_3.3_spmd, %region_4.5_spmd} | conditional | flops 134351360 | bytes 3422258 | solution.py:50
  80.7 13.8 %conditional.6 = (f32[6144,256]{1,0:T(8,128)}) conditional(s32[]{:T(128)} %bitcast.62, f32[6144,256]{1,0:T(8,128)} %get-tuple-element.664, (s32[16,512]{1,0:T(8,128)}, s32[]{:T(128)}, bf16[16,512,512]{2,1,0:T(8,128)(2,1)}, bf16[6144,256]{1,0:T(8,128)(2,1)S(1)}, f32[6144,256]{1,0:T(8,128)}) %tuple.128), branch_computations={%region_3.3_spmd, %region_4.5_spmd} | conditional | flops 134351360 | bytes 3422258 | solution.py:50
  95.7 13.8 %conditional.6 = (f32[6144,256]{1,0:T(8,128)}) conditional(s32[]{:T(128)} %bitcast.62, f32[6144,256]{1,0:T(8,128)} %get-tuple-element.664, (s32[16,512]{1,0:T(8,128)}, s32[]{:T(128)}, bf16[16,512,512]{2,1,0:T(8,128)(2,1)}, bf16[6144,256]{1,0:T(8,128)(2,1)S(1)}, f32[6144,256]{1,0:T(8,128)}) %tuple.128), branch_computations={%region_3.3_spmd, %region_4.5_spmd} | conditional | flops 134351360 | bytes 3422258 | solution.py:50
  129.3 166.7 %collective-permute-start.2 = (f32[384,256]{1,0:T(8,128)S(1)}, f32[384,256]{1,0:T(8,128)S(1)}, u32[]{:S(2)}, u32[]{:S(2)}) collective-permute-start(f32[384,256]{1,0:T(8,128)S(1)} %gather_fusion.6), channel_id=1, source_target_pairs={{0,1},{1,2},{2,3},{3,4},{4,5},{5,6},{6,7},{7,8},{8,9},{9,10},{10,1... | collective-permute-start | bytes 1179656 | tf_op jit(solution)/shard_map/ppermute | solution.py:10
  326.9 75.4 %while.50 = (s32[]{:T(128)}, f32[6144,256]{1,0:T(8,128)}, pred[16]{0:T(512)(128)(4,1)S(1)}, s32[16,512]{1,0:T(8,128)}, bf16[16,512,512]{2,1,0:T(8,128)(2,1)}, /*index=5*/bf16[6144,256]{1,0:T(8,128)(2,1)S(1)}, s32[]{:T(128)}) while((s32[]{:T(128)}, f32[6144,256]{1,0:T(8,128)}, pred[16]{0:T(512)(128)(4,1)S(1)}, s32[16,512]{1,0:T(8,128)}, ...), condition=%wide.region_13.14_spmd, body=%wide.region_9.13_spmd.sunk | while | flops 134351360 | bytes 3422386 | solution.py:52
  328.1 13.8 %conditional.7 = (f32[6144,256]{1,0:T(8,128)}) conditional(s32[]{:T(128)} %bitcast.63, f32[6144,256]{1,0:T(8,128)} %get-tuple-element.685, (s32[16,512]{1,0:T(8,128)}, s32[]{:T(128)}, bf16[16,512,512]{2,1,0:T(8,128)(2,1)}, bf16[6144,256]{1,0:T(8,128)(2,1)S(1)}, f32[6144,256]{1,0:T(8,128)}) %tuple.130), branch_computations={%region_10.10_spmd, %region_11.12_spmd} | conditional | flops 134351360 | bytes 3422258 | solution.py:50
  343.1 13.8 %conditional.7 = (f32[6144,256]{1,0:T(8,128)}) conditional(s32[]{:T(128)} %bitcast.63, f32[6144,256]{1,0:T(8,128)} %get-tuple-element.685, (s32[16,512]{1,0:T(8,128)}, s32[]{:T(128)}, bf16[16,512,512]{2,1,0:T(8,128)(2,1)}, bf16[6144,256]{1,0:T(8,128)(2,1)S(1)}, f32[6144,256]{1,0:T(8,128)}) %tuple.130), branch_computations={%region_10.10_spmd, %region_11.12_spmd} | conditional | flops 134351360 | bytes 3422258 | solution.py:50
  358.1 13.8 %conditional.7 = (f32[6144,256]{1,0:T(8,128)}) conditional(s32[]{:T(128)} %bitcast.63, f32[6144,256]{1,0:T(8,128)} %get-tuple-element.685, (s32[16,512]{1,0:T(8,128)}, s32[]{:T(128)}, bf16[16,512,512]{2,1,0:T(8,128)(2,1)}, bf16[6144,256]{1,0:T(8,128)(2,1)S(1)}, f32[6144,256]{1,0:T(8,128)}) %tuple.130), branch_computations={%region_10.10_spmd, %region_11.12_spmd} | conditional | flops 134351360 | bytes 3422258 | solution.py:50
  373.1 13.8 %conditional.7 = (f32[6144,256]{1,0:T(8,128)}) conditional(s32[]{:T(128)} %bitcast.63, f32[6144,256]{1,0:T(8,128)} %get-tuple-element.685, (s32[16,512]{1,0:T(8,128)}, s32[]{:T(128)}, bf16[16,512,512]{2,1,0:T(8,128)(2,1)}, bf16[6144,256]{1,0:T(8,128)(2,1)S(1)}, f32[6144,256]{1,0:T(8,128)}) %tuple.130), branch_computations={%region_10.10_spmd, %region_11.12_spmd} | conditional | flops 134351360 | bytes 3422258 | solution.py:50
  406.8 167.9 %collective-permute-start.4 = (f32[384,256]{1,0:T(8,128)S(1)}, f32[384,256]{1,0:T(8,128)S(1)}, u32[]{:S(2)}, u32[]{:S(2)}) collective-permute-start(f32[384,256]{1,0:T(8,128)S(1)} %gather_fusion.8), channel_id=1, source_target_pairs={{0,1},{1,2},{2,3},{3,4},{4,5},{5,6},{6,7},{7,8},{8,9},{9,10},{10,1... | collective-permute-start | bytes 1179656 | tf_op jit(solution)/shard_map/ppermute | solution.py:10
  606.9 75.5 %while.51 = (s32[]{:T(128)}, f32[6144,256]{1,0:T(8,128)}, pred[16]{0:T(512)(128)(4,1)S(1)}, s32[16,512]{1,0:T(8,128)}, bf16[16,512,512]{2,1,0:T(8,128)(2,1)}, /*index=5*/bf16[6144,256]{1,0:T(8,128)(2,1)S(1)}, s32[]{:T(128)}) while((s32[]{:T(128)}, f32[6144,256]{1,0:T(8,128)}, pred[16]{0:T(512)(128)(4,1)S(1)}, s32[16,512]{1,0:T(8,128)}, ...), condition=%wide.region_20.21_spmd, body=%wide.region_16.20_spmd.sunk | while | flops 134351360 | bytes 3422386 | solution.py:52
  608.1 13.8 %conditional.8 = (f32[6144,256]{1,0:T(8,128)}) conditional(s32[]{:T(128)} %bitcast.64, f32[6144,256]{1,0:T(8,128)} %get-tuple-element.706, (s32[16,512]{1,0:T(8,128)}, s32[]{:T(128)}, bf16[16,512,512]{2,1,0:T(8,128)(2,1)}, bf16[6144,256]{1,0:T(8,128)(2,1)S(1)}, f32[6144,256]{1,0:T(8,128)}) %tuple.132), branch_computations={%region_17.17_spmd, %region_18.19_spmd} | conditional | flops 134351360 | bytes 3422258 | solution.py:50
  623.2 13.8 %conditional.8 = (f32[6144,256]{1,0:T(8,128)}) conditional(s32[]{:T(128)} %bitcast.64, f32[6144,256]{1,0:T(8,128)} %get-tuple-element.706, (s32[16,512]{1,0:T(8,128)}, s32[]{:T(128)}, bf16[16,512,512]{2,1,0:T(8,128)(2,1)}, bf16[6144,256]{1,0:T(8,128)(2,1)S(1)}, f32[6144,256]{1,0:T(8,128)}) %tuple.132), branch_computations={%region_17.17_spmd, %region_18.19_spmd} | conditional | flops 134351360 | bytes 3422258 | solution.py:50
  638.2 13.8 %conditional.8 = (f32[6144,256]{1,0:T(8,128)}) conditional(s32[]{:T(128)} %bitcast.64, f32[6144,256]{1,0:T(8,128)} %get-tuple-element.706, (s32[16,512]{1,0:T(8,128)}, s32[]{:T(128)}, bf16[16,512,512]{2,1,0:T(8,128)(2,1)}, bf16[6144,256]{1,0:T(8,128)(2,1)S(1)}, f32[6144,256]{1,0:T(8,128)}) %tuple.132), branch_computations={%region_17.17_spmd, %region_18.19_spmd} | conditional | flops 134351360 | bytes 3422258 | solution.py:50
  653.3 13.8 %conditional.8 = (f32[6144,256]{1,0:T(8,128)}) conditional(s32[]{:T(128)} %bitcast.64, f32[6144,256]{1,0:T(8,128)} %get-tuple-element.706, (s32[16,512]{1,0:T(8,128)}, s32[]{:T(128)}, bf16[16,512,512]{2,1,0:T(8,128)(2,1)}, bf16[6144,256]{1,0:T(8,128)(2,1)S(1)}, f32[6144,256]{1,0:T(8,128)}) %tuple.132), branch_computations={%region_17.17_spmd, %region_18.19_spmd} | conditional | flops 134351360 | bytes 3422258 | solution.py:50
  691.4 168.4 %collective-permute-start.6 = (f32[384,256]{1,0:T(8,128)S(1)}, f32[384,256]{1,0:T(8,128)S(1)}, u32[]{:S(2)}, u32[]{:S(2)}) collective-permute-start(f32[384,256]{1,0:T(8,128)S(1)} %gather_fusion.10), channel_id=1, source_target_pairs={{0,1},{1,2},{2,3},{3,4},{4,5},{5,6},{6,7},{7,8},{8,9},{9,10},{10,1... | collective-permute-start | bytes 1179656 | tf_op jit(solution)/shard_map/ppermute | solution.py:10
  892.0 12.9 %fusion.13 = f32[256,256]{0,1:T(8,128)} fusion(f32[6144,256]{1,0:T(8,128)S(1)} %multiply_subtract_fusion, pred[6144]{0:T(1024)(128)(4,1)S(1)} %not_and_fusion), kind=kOutput, calls=%fused_computation.47 | convolution fusion | flops 4833411072 | bytes 6559744 | tf_op jit(solution)/shard_map/dot_general | solution.py:67
  906.2 132.1 %all-reduce.3.cloned.1.call-done = f32[256,256]{0,1:T(8,128)} async-done(((f32[256,256]{0,1:T(8,128)}), f32[256,256]{0,1:T(8,128)}) %all-reduce.3.cloned.1.call-update) | async-done | bytes 262160 | tf_op jit(solution)/shard_map/psum | solution.py:74
  1040.8 11.7 %cholesky.50 = f32[128,128]{1,0:T(8,128)S(1)} custom-call(f32[128,128]{1,0:T(8,128)S(1)} %cholesky.118), custom_call_target="Cholesky" | custom-call | tf_op jit(solution)/shard_map/jit(cholesky)/cholesky | solution.py:77
  1052.6 9.8 custom-call.15
  1062.8 11.7 %cholesky.105 = f32[128,128]{1,0:T(8,128)S(1)} custom-call(f32[128,128]{1,0:T(8,128)S(1)} %convolution_subtract_fusion.1), custom_call_target="Cholesky" | custom-call | tf_op jit(solution)/shard_map/jit(cholesky)/cholesky | solution.py:77
  1080.4 19.8 %custom-call.16 = f32[2,128,128]{1,2,0:T(8,128)S(1)} custom-call(f32[2,128,128]{2,1,0:T(8,128)S(1)} %get-tuple-element.459), custom_call_target="InvertDiagBlocksLowerTriangular" | custom-call | tf_op jit(solution)/shard_map/jit(_solve_triangular)/triangular_solve | solution.py:78
  (229 shorter events, 371.4 us)
Async XLA Ops:
  6.5 1031.7 %all-reduce.3.cloned.1.call-start = ((), (), s32[]{:S(2)}) async-start(), calls=%async_computation | async-start | bytes 524288 | tf_op jit(solution)/shard_map/psum | solution.py:74
  7.3 5.8 copy-start.1
  15.7 14.6 %collective-permute-start = (f32[384]{0:T(512)S(1)}, f32[384]{0:T(512)S(1)}, u32[]{:S(2)}, u32[]{:S(2)}) collective-permute-start(f32[384]{0:T(512)S(1)} %gather_fusion.3), channel_id=1, source_target_pairs={{0,1},{1,2},{2,3},{3,4},{4,5},{5,6},{6,7},{7,8},{8,9},{9,10},{10,1... | collective-permute-start | bytes 4616 | tf_op jit(solution)/shard_map/ppermute | solution.py:10
  22.5 10.8 collective-permute-start.1
  129.3 173.0 %collective-permute-start.2 = (f32[384,256]{1,0:T(8,128)S(1)}, f32[384,256]{1,0:T(8,128)S(1)}, u32[]{:S(2)}, u32[]{:S(2)}) collective-permute-start(f32[384,256]{1,0:T(8,128)S(1)} %gather_fusion.6), channel_id=1, source_target_pairs={{0,1},{1,2},{2,3},{3,4},{4,5},{5,6},{6,7},{7,8},{8,9},{9,10},{10,1... | collective-permute-start | bytes 1179656 | tf_op jit(solution)/shard_map/ppermute | solution.py:10
  300.5 9.6 collective-permute-start.3
  406.8 173.7 %collective-permute-start.4 = (f32[384,256]{1,0:T(8,128)S(1)}, f32[384,256]{1,0:T(8,128)S(1)}, u32[]{:S(2)}, u32[]{:S(2)}) collective-permute-start(f32[384,256]{1,0:T(8,128)S(1)} %gather_fusion.8), channel_id=1, source_target_pairs={{0,1},{1,2},{2,3},{3,4},{4,5},{5,6},{6,7},{7,8},{8,9},{9,10},{10,1... | collective-permute-start | bytes 1179656 | tf_op jit(solution)/shard_map/ppermute | solution.py:10
  579.1 9.3 collective-permute-start.5
  682.4 179.5 %copy-start.2 = (s32[32]{0:T(128)S(1)}, s32[32]{0:T(128)}, u32[]{:S(2)}) copy-start(s32[32]{0:T(128)} %param.24) | copy-start | bytes 388
  691.4 172.4 %collective-permute-start.6 = (f32[384,256]{1,0:T(8,128)S(1)}, f32[384,256]{1,0:T(8,128)S(1)}, u32[]{:S(2)}, u32[]{:S(2)}) collective-permute-start(f32[384,256]{1,0:T(8,128)S(1)} %gather_fusion.10), channel_id=1, source_target_pairs={{0,1},{1,2},{2,3},{3,4},{4,5},{5,6},{6,7},{7,8},{8,9},{9,10},{10,1... | collective-permute-start | bytes 1179656 | tf_op jit(solution)/shard_map/ppermute | solution.py:10
  859.7 12.0 %collective-permute-start.7 = (f32[384,256]{1,0:T(8,128)S(1)}, f32[384,256]{1,0:T(8,128)S(1)}, u32[]{:S(2)}, u32[]{:S(2)}) collective-permute-start(f32[384,256]{1,0:T(8,128)S(1)} %gather_fusion.11), channel_id=1, source_target_pairs={{1,0},{2,1},{3,2},{4,3},{5,4},{6,5},{7,6},{8,7},{9,8},{10,9},{11,1... | collective-permute-start | bytes 1179656 | tf_op jit(solution)/shard_map/ppermute | solution.py:10
  889.3 2.7 copy-start
Sparse Core Ops, SparseCore 0:
  905.0 133.2 all-reduce.2
where the time goes:
time: 1140 us; the launch traced here: 1120 us
  starting transfers between devices  514 us (45%)
  other arithmetic  258 us (23%)
  waiting for transfers between devices  132 us (12%)
  local copies, waits for them, and re-layouts  115 us (10%)
  matrix products  48.7 us (4%)
  loops' own time  32.5 us (3%)
  between operations  16.5 us (1%)
    ppermute x8, starting transfers between devices, passed_along(): return lax.ppermute(block, axis, route)  514 us
    psum x1, waiting for transfers between devices, body(): gram = lax.psum(partial_value, 'mesh')  132 us
    scatter-add x12, other arithmetic, compute(): return acc.at[rows].add(part)  107 us
    scatter-add x6, other arithmetic, ham(): local.at[lower_rows].add(coming_up).at[upper_rows].add(coming_down)  47.2 us
    another operation x6, other arithmetic, body(): factor = jnp.linalg.cholesky(gram)  34 us
    another operation x3, loops' own time, ham(): local = lax.fori_loop(0, slots, add_element, empty)  31.5 us
    dynamic_slice x48, local copies, waits for them, and re-layouts, add_element(): return lax.cond(slot_live[slot], compute, lambda acc: acc, total)  28.8 us
    dot_general x12, matrix products, compute(): jnp.dot(element_blocks[slot], scaled[rows], preferred_element_type=jnp.fl...  25.6 us
  transfers between devices with their start and end apart: 9, of which 1 were waited for; matrix products, arithmetic and copies ran while one was open for 4% of the time, Pallas kernels for 0%

commit v1 on v0

--- a/solution.py
+++ b/solution.py
@@ -71,7 +71,8 @@
         precision=lax.Precision.HIGHEST,
         preferred_element_type=jnp.float32,
     )
-    gram = lax.psum(partial_value, "mesh")
+    start_frame = lambda own_rows: lax.all_gather(own_rows, "mesh").sum(axis=0)
+    gram = start_frame(partial_value)
     total = (jnp.sum(node_counts) - shared * (devices - 1)).astype(jnp.float32)
     gram = gram / total
     factor = jnp.linalg.cholesky(gram)

time: 1140 us -> 1090 us (0.956)
  waiting for transfers between devices: 132 us -> 83.2 us
    psum x1 -> x0, waiting for transfers between devices: 132 us -> none  [body(): gram = lax.psum(partial_value, 'mesh')]
    all_gather x0 -> x1, waiting for transfers between devices: none -> 83.1 us  [body(): start_frame = lambda own_rows: lax.all_gather(own_rows, 'mesh').sum(axis=0)]
where the time goes in v1:
time: 1090 us; the launch traced here: 1070 us
  starting transfers between devices  514 us (47%)
  other arithmetic  261 us (24%)
  local copies, waits for them, and re-layouts  115 us (11%)
  waiting for transfers between devices  83.2 us (8%)
  matrix products  48.3 us (4%)
  loops' own time  32.5 us (3%)
  between operations  16.9 us (2%)
    ppermute x8, starting transfers between devices, passed_along(): return lax.ppermute(block, axis, route)  514 us
    scatter-add x12, other arithmetic, compute(): return acc.at[rows].add(part)  107 us
    all_gather x1, waiting for transfers between devices, body(): start_frame = lambda own_rows: lax.all_gather(own_rows, 'mesh').sum(axis=0)  83.1 us
    scatter-add x6, other arithmetic, ham(): local.at[lower_rows].add(coming_up).at[upper_rows].add(coming_down)  47.4 us
    another operation x6, other arithmetic, body(): factor = jnp.linalg.cholesky(gram)  34 us
    another operation x3, loops' own time, ham(): local = lax.fori_loop(0, slots, add_element, empty)  31.5 us
    dynamic_slice x48, local copies, waits for them, and re-layouts, add_element(): return lax.cond(slot_live[slot], compute, lambda acc: acc, total)  28.8 us
    dot_general x12, matrix products, compute(): jnp.dot(element_blocks[slot], scaled[rows], preferred_element_type=jnp.fl...  25.6 us
  transfers between devices with their start and end apart: 9, of which 1 were waited for; matrix products, arithmetic and copies ran while one was open for 4% of the time, Pallas kernels for 0%

profile of v1, /device:TPU:0, one launch (start us, length us, event | category | flops | bytes accessed | tf_op | source)
XLA Modules:
  0.0 1070.3 jit_solution(3935579334490655620)
XLA Ops:
  49.4 75.4 %while.49 = (s32[]{:T(128)}, f32[6144,256]{1,0:T(8,128)}, pred[16]{0:T(512)(128)(4,1)S(1)}, s32[16,512]{1,0:T(8,128)}, bf16[16,512,512]{2,1,0:T(8,128)(2,1)}, /*index=5*/bf16[6144,256]{1,0:T(8,128)(2,1)S(1)}, s32[]{:T(128)}) while((s32[]{:T(128)}, f32[6144,256]{1,0:T(8,128)}, pred[16]{0:T(512)(128)(4,1)S(1)}, s32[16,512]{1,0:T(8,128)}, ...), condition=%wide.region_6.7_spmd, body=%wide.region_2.6_spmd.sunk | while | flops 134351360 | bytes 3422386 | solution.py:52
  50.7 13.8 %conditional.6 = (f32[6144,256]{1,0:T(8,128)}) conditional(s32[]{:T(128)} %bitcast.63, f32[6144,256]{1,0:T(8,128)} %get-tuple-element.664, (s32[16,512]{1,0:T(8,128)}, s32[]{:T(128)}, bf16[16,512,512]{2,1,0:T(8,128)(2,1)}, bf16[6144,256]{1,0:T(8,128)(2,1)S(1)}, f32[6144,256]{1,0:T(8,128)}) %tuple.128), branch_computations={%region_3.3_spmd, %region_4.5_spmd} | conditional | flops 134351360 | bytes 3422258 | solution.py:50
  65.7 13.8 %conditional.6 = (f32[6144,256]{1,0:T(8,128)}) conditional(s32[]{:T(128)} %bitcast.63, f32[6144,256]{1,0:T(8,128)} %get-tuple-element.664, (s32[16,512]{1,0:T(8,128)}, s32[]{:T(128)}, bf16[16,512,512]{2,1,0:T(8,128)(2,1)}, bf16[6144,256]{1,0:T(8,128)(2,1)S(1)}, f32[6144,256]{1,0:T(8,128)}) %tuple.128), branch_computations={%region_3.3_spmd, %region_4.5_spmd} | conditional | flops 134351360 | bytes 3422258 | solution.py:50
  80.7 13.8 %conditional.6 = (f32[6144,256]{1,0:T(8,128)}) conditional(s32[]{:T(128)} %bitcast.63, f32[6144,256]{1,0:T(8,128)} %get-tuple-element.664, (s32[16,512]{1,0:T(8,128)}, s32[]{:T(128)}, bf16[16,512,512]{2,1,0:T(8,128)(2,1)}, bf16[6144,256]{1,0:T(8,128)(2,1)S(1)}, f32[6144,256]{1,0:T(8,128)}) %tuple.128), branch_computations={%region_3.3_spmd, %region_4.5_spmd} | conditional | flops 134351360 | bytes 3422258 | solution.py:50
  95.7 13.8 %conditional.6 = (f32[6144,256]{1,0:T(8,128)}) conditional(s32[]{:T(128)} %bitcast.63, f32[6144,256]{1,0:T(8,128)} %get-tuple-element.664, (s32[16,512]{1,0:T(8,128)}, s32[]{:T(128)}, bf16[16,512,512]{2,1,0:T(8,128)(2,1)}, bf16[6144,256]{1,0:T(8,128)(2,1)S(1)}, f32[6144,256]{1,0:T(8,128)}) %tuple.128), branch_computations={%region_3.3_spmd, %region_4.5_spmd} | conditional | flops 134351360 | bytes 3422258 | solution.py:50
  129.3 166.7 %collective-permute-start.2 = (f32[384,256]{1,0:T(8,128)S(1)}, f32[384,256]{1,0:T(8,128)S(1)}, u32[]{:S(2)}, u32[]{:S(2)}) collective-permute-start(f32[384,256]{1,0:T(8,128)S(1)} %gather_fusion.6), channel_id=1, source_target_pairs={{0,1},{1,2},{2,3},{3,4},{4,5},{5,6},{6,7},{7,8},{8,9},{9,10},{10,1... | collective-permute-start | bytes 1179656 | tf_op jit(solution)/shard_map/ppermute | solution.py:10
  326.6 75.4 %while.50 = (s32[]{:T(128)}, f32[6144,256]{1,0:T(8,128)}, pred[16]{0:T(512)(128)(4,1)S(1)}, s32[16,512]{1,0:T(8,128)}, bf16[16,512,512]{2,1,0:T(8,128)(2,1)}, /*index=5*/bf16[6144,256]{1,0:T(8,128)(2,1)S(1)}, s32[]{:T(128)}) while((s32[]{:T(128)}, f32[6144,256]{1,0:T(8,128)}, pred[16]{0:T(512)(128)(4,1)S(1)}, s32[16,512]{1,0:T(8,128)}, ...), condition=%wide.region_13.14_spmd, body=%wide.region_9.13_spmd.sunk | while | flops 134351360 | bytes 3422386 | solution.py:52
  327.8 13.8 %conditional.7 = (f32[6144,256]{1,0:T(8,128)}) conditional(s32[]{:T(128)} %bitcast.64, f32[6144,256]{1,0:T(8,128)} %get-tuple-element.685, (s32[16,512]{1,0:T(8,128)}, s32[]{:T(128)}, bf16[16,512,512]{2,1,0:T(8,128)(2,1)}, bf16[6144,256]{1,0:T(8,128)(2,1)S(1)}, f32[6144,256]{1,0:T(8,128)}) %tuple.130), branch_computations={%region_10.10_spmd, %region_11.12_spmd} | conditional | flops 134351360 | bytes 3422258 | solution.py:50
  342.8 13.8 %conditional.7 = (f32[6144,256]{1,0:T(8,128)}) conditional(s32[]{:T(128)} %bitcast.64, f32[6144,256]{1,0:T(8,128)} %get-tuple-element.685, (s32[16,512]{1,0:T(8,128)}, s32[]{:T(128)}, bf16[16,512,512]{2,1,0:T(8,128)(2,1)}, bf16[6144,256]{1,0:T(8,128)(2,1)S(1)}, f32[6144,256]{1,0:T(8,128)}) %tuple.130), branch_computations={%region_10.10_spmd, %region_11.12_spmd} | conditional | flops 134351360 | bytes 3422258 | solution.py:50
  357.8 13.8 %conditional.7 = (f32[6144,256]{1,0:T(8,128)}) conditional(s32[]{:T(128)} %bitcast.64, f32[6144,256]{1,0:T(8,128)} %get-tuple-element.685, (s32[16,512]{1,0:T(8,128)}, s32[]{:T(128)}, bf16[16,512,512]{2,1,0:T(8,128)(2,1)}, bf16[6144,256]{1,0:T(8,128)(2,1)S(1)}, f32[6144,256]{1,0:T(8,128)}) %tuple.130), branch_computations={%region_10.10_spmd, %region_11.12_spmd} | conditional | flops 134351360 | bytes 3422258 | solution.py:50
  372.9 13.8 %conditional.7 = (f32[6144,256]{1,0:T(8,128)}) conditional(s32[]{:T(128)} %bitcast.64, f32[6144,256]{1,0:T(8,128)} %get-tuple-element.685, (s32[16,512]{1,0:T(8,128)}, s32[]{:T(128)}, bf16[16,512,512]{2,1,0:T(8,128)(2,1)}, bf16[6144,256]{1,0:T(8,128)(2,1)S(1)}, f32[6144,256]{1,0:T(8,128)}) %tuple.130), branch_computations={%region_10.10_spmd, %region_11.12_spmd} | conditional | flops 134351360 | bytes 3422258 | solution.py:50
  406.5 167.9 %collective-permute-start.4 = (f32[384,256]{1,0:T(8,128)S(1)}, f32[384,256]{1,0:T(8,128)S(1)}, u32[]{:S(2)}, u32[]{:S(2)}) collective-permute-start(f32[384,256]{1,0:T(8,128)S(1)} %gather_fusion.8), channel_id=1, source_target_pairs={{0,1},{1,2},{2,3},{3,4},{4,5},{5,6},{6,7},{7,8},{8,9},{9,10},{10,1... | collective-permute-start | bytes 1179656 | tf_op jit(solution)/shard_map/ppermute | solution.py:10
  607.5 75.5 %while.51 = (s32[]{:T(128)}, f32[6144,256]{1,0:T(8,128)}, pred[16]{0:T(512)(128)(4,1)S(1)}, s32[16,512]{1,0:T(8,128)}, bf16[16,512,512]{2,1,0:T(8,128)(2,1)}, /*index=5*/bf16[6144,256]{1,0:T(8,128)(2,1)S(1)}, s32[]{:T(128)}) while((s32[]{:T(128)}, f32[6144,256]{1,0:T(8,128)}, pred[16]{0:T(512)(128)(4,1)S(1)}, s32[16,512]{1,0:T(8,128)}, ...), condition=%wide.region_20.21_spmd, body=%wide.region_16.20_spmd.sunk | while | flops 134351360 | bytes 3422386 | solution.py:52
  608.7 13.8 %conditional.8 = (f32[6144,256]{1,0:T(8,128)}) conditional(s32[]{:T(128)} %bitcast.65, f32[6144,256]{1,0:T(8,128)} %get-tuple-element.706, (s32[16,512]{1,0:T(8,128)}, s32[]{:T(128)}, bf16[16,512,512]{2,1,0:T(8,128)(2,1)}, bf16[6144,256]{1,0:T(8,128)(2,1)S(1)}, f32[6144,256]{1,0:T(8,128)}) %tuple.132), branch_computations={%region_17.17_spmd, %region_18.19_spmd} | conditional | flops 134351360 | bytes 3422258 | solution.py:50
  623.7 13.8 %conditional.8 = (f32[6144,256]{1,0:T(8,128)}) conditional(s32[]{:T(128)} %bitcast.65, f32[6144,256]{1,0:T(8,128)} %get-tuple-element.706, (s32[16,512]{1,0:T(8,128)}, s32[]{:T(128)}, bf16[16,512,512]{2,1,0:T(8,128)(2,1)}, bf16[6144,256]{1,0:T(8,128)(2,1)S(1)}, f32[6144,256]{1,0:T(8,128)}) %tuple.132), branch_computations={%region_17.17_spmd, %region_18.19_spmd} | conditional | flops 134351360 | bytes 3422258 | solution.py:50
  638.8 13.8 %conditional.8 = (f32[6144,256]{1,0:T(8,128)}) conditional(s32[]{:T(128)} %bitcast.65, f32[6144,256]{1,0:T(8,128)} %get-tuple-element.706, (s32[16,512]{1,0:T(8,128)}, s32[]{:T(128)}, bf16[16,512,512]{2,1,0:T(8,128)(2,1)}, bf16[6144,256]{1,0:T(8,128)(2,1)S(1)}, f32[6144,256]{1,0:T(8,128)}) %tuple.132), branch_computations={%region_17.17_spmd, %region_18.19_spmd} | conditional | flops 134351360 | bytes 3422258 | solution.py:50
  653.8 13.8 %conditional.8 = (f32[6144,256]{1,0:T(8,128)}) conditional(s32[]{:T(128)} %bitcast.65, f32[6144,256]{1,0:T(8,128)} %get-tuple-element.706, (s32[16,512]{1,0:T(8,128)}, s32[]{:T(128)}, bf16[16,512,512]{2,1,0:T(8,128)(2,1)}, bf16[6144,256]{1,0:T(8,128)(2,1)S(1)}, f32[6144,256]{1,0:T(8,128)}) %tuple.132), branch_computations={%region_17.17_spmd, %region_18.19_spmd} | conditional | flops 134351360 | bytes 3422258 | solution.py:50
  691.9 168.4 %collective-permute-start.6 = (f32[384,256]{1,0:T(8,128)S(1)}, f32[384,256]{1,0:T(8,128)S(1)}, u32[]{:S(2)}, u32[]{:S(2)}) collective-permute-start(f32[384,256]{1,0:T(8,128)S(1)} %gather_fusion.10), channel_id=1, source_target_pairs={{0,1},{1,2},{2,3},{3,4},{4,5},{5,6},{6,7},{7,8},{8,9},{9,10},{10,1... | collective-permute-start | bytes 1179656 | tf_op jit(solution)/shard_map/ppermute | solution.py:10
  891.3 12.5 %fusion.13 = f32[256,256]{1,0:T(8,128)} fusion(f32[6144,256]{1,0:T(8,128)S(1)} %multiply_subtract_fusion, pred[6144]{0:T(1024)(128)(4,1)S(1)} %not_and_fusion), kind=kOutput, calls=%fused_computation.47 | convolution fusion | flops 4833411072 | bytes 6559744 | tf_op jit(solution)/shard_map/dot_general | solution.py:67
  905.8 83.1 %all-gather.3.cloned.1.call-done = f32[8192,256]{1,0:T(8,128)} async-done(((f32[256,256]{1,0:T(8,128)}), f32[8192,256]{1,0:T(8,128)}) %all-gather.3.cloned.1.call-update) | async-done | bytes 8388624 | tf_op jit(solution)/shard_map/all_gather | solution.py:74
  993.4 11.7 %cholesky.50 = f32[128,128]{1,0:T(8,128)S(1)} custom-call(f32[128,128]{1,0:T(8,128)S(1)} %cholesky.118), custom_call_target="Cholesky" | custom-call | tf_op jit(solution)/shard_map/jit(cholesky)/cholesky | solution.py:78
  1005.2 9.8 custom-call.15
  1015.5 11.7 %cholesky.105 = f32[128,128]{1,0:T(8,128)S(1)} custom-call(f32[128,128]{1,0:T(8,128)S(1)} %convolution_subtract_fusion.1), custom_call_target="Cholesky" | custom-call | tf_op jit(solution)/shard_map/jit(cholesky)/cholesky | solution.py:78
  1033.3 19.9 %custom-call.16 = f32[2,128,128]{1,2,0:T(8,128)S(1)} custom-call(f32[2,128,128]{2,1,0:T(8,128)S(1)} %get-tuple-element.459), custom_call_target="InvertDiagBlocksLowerTriangular" | custom-call | tf_op jit(solution)/shard_map/jit(_solve_triangular)/triangular_solve | solution.py:79
  (231 shorter events, 373.6 us)
Async XLA Ops:
  6.5 982.4 %all-gather.3.cloned.1.call-start = ((), (), s32[]{:S(2)}) async-start(), calls=%async_computation | async-start | bytes 8650752 | tf_op jit(solution)/shard_map/all_gather | solution.py:74
  7.3 5.8 copy-start.1
  15.7 14.6 %collective-permute-start = (f32[384]{0:T(512)S(1)}, f32[384]{0:T(512)S(1)}, u32[]{:S(2)}, u32[]{:S(2)}) collective-permute-start(f32[384]{0:T(512)S(1)} %gather_fusion.3), channel_id=1, source_target_pairs={{0,1},{1,2},{2,3},{3,4},{4,5},{5,6},{6,7},{7,8},{8,9},{9,10},{10,1... | collective-permute-start | bytes 4616 | tf_op jit(solution)/shard_map/ppermute | solution.py:10
  22.5 10.8 %collective-permute-start.1 = (f32[384,256]{1,0:T(8,128)S(1)}, f32[384,256]{1,0:T(8,128)S(1)}, u32[]{:S(2)}, u32[]{:S(2)}) collective-permute-start(f32[384,256]{1,0:T(8,128)S(1)} %gather_fusion.5), channel_id=1, source_target_pairs={{0,1},{1,2},{2,3},{3,4},{4,5},{5,6},{6,7},{7,8},{8,9},{9,10},{10,1... | collective-permute-start | bytes 1179656 | tf_op jit(solution)/shard_map/ppermute | solution.py:10
  129.3 172.7 %collective-permute-start.2 = (f32[384,256]{1,0:T(8,128)S(1)}, f32[384,256]{1,0:T(8,128)S(1)}, u32[]{:S(2)}, u32[]{:S(2)}) collective-permute-start(f32[384,256]{1,0:T(8,128)S(1)} %gather_fusion.6), channel_id=1, source_target_pairs={{0,1},{1,2},{2,3},{3,4},{4,5},{5,6},{6,7},{7,8},{8,9},{9,10},{10,1... | collective-permute-start | bytes 1179656 | tf_op jit(solution)/shard_map/ppermute | solution.py:10
  300.5 9.3 collective-permute-start.3
  402.0 178.2 %copy-start.2 = (s32[32]{0:T(128)S(1)}, s32[32]{0:T(128)}, u32[]{:S(2)}) copy-start(s32[32]{0:T(128)} %param.24) | copy-start | bytes 388
  406.5 174.3 %collective-permute-start.4 = (f32[384,256]{1,0:T(8,128)S(1)}, f32[384,256]{1,0:T(8,128)S(1)}, u32[]{:S(2)}, u32[]{:S(2)}) collective-permute-start(f32[384,256]{1,0:T(8,128)S(1)} %gather_fusion.8), channel_id=1, source_target_pairs={{0,1},{1,2},{2,3},{3,4},{4,5},{5,6},{6,7},{7,8},{8,9},{9,10},{10,1... | collective-permute-start | bytes 1179656 | tf_op jit(solution)/shard_map/ppermute | solution.py:10
  578.9 10.2 collective-permute-start.5
  691.9 171.2 %collective-permute-start.6 = (f32[384,256]{1,0:T(8,128)S(1)}, f32[384,256]{1,0:T(8,128)S(1)}, u32[]{:S(2)}, u32[]{:S(2)}) collective-permute-start(f32[384,256]{1,0:T(8,128)S(1)} %gather_fusion.10), channel_id=1, source_target_pairs={{0,1},{1,2},{2,3},{3,4},{4,5},{5,6},{6,7},{7,8},{8,9},{9,10},{10,1... | collective-permute-start | bytes 1179656 | tf_op jit(solution)/shard_map/ppermute | solution.py:10
  860.3 10.7 %collective-permute-start.7 = (f32[384,256]{1,0:T(8,128)S(1)}, f32[384,256]{1,0:T(8,128)S(1)}, u32[]{:S(2)}, u32[]{:S(2)}) collective-permute-start(f32[384,256]{1,0:T(8,128)S(1)} %gather_fusion.11), channel_id=1, source_target_pairs={{1,0},{2,1},{3,2},{4,3},{5,4},{6,5},{7,6},{8,7},{9,8},{10,9},{11,1... | collective-permute-start | bytes 1179656 | tf_op jit(solution)/shard_map/ppermute | solution.py:10
  888.6 2.7 copy-start
Sparse Core Ops, SparseCore 0:
  903.9 84.9 all-gather.2
